TPU v7x, 32 devices: a whole 2x2x4 slice. The times are simulated.
32 devices in a mesh: dp: 4 (over z), ctx: 8 (over y, x, core).
Axes of the slice: x: 2, y: 2, z: 4, core: 2. Of those that a mesh axis runs over, the one named last changes fastest.
Arguments:
- queries: bfloat16 [4, 1024, 1024], P('dp', 'ctx'), may hold values from -6 to 6
- keys: bfloat16 [4, 1024, 1024], P('dp', 'ctx'), may hold values from -6 to 6
- values: bfloat16 [4, 1024, 1024], P('dp', 'ctx'), may hold values from -6 to 6
- outputs: bfloat16 [4, 1024, 1024], P('dp', 'ctx'), may hold values from -1.25 to 1.25
- d_out: bfloat16 [4, 1024, 1024], P('dp', 'ctx'), may hold values from -6 to 6
- lse: float32 [4, 16, 1024], P('dp', None, 'ctx'), may hold values from 3 to 5
- glob_keys: bfloat16 [128, 1024], replicated, may hold values from -6 to 6
- glob_values: bfloat16 [128, 1024], replicated, may hold values from -6 to 6
- rand_owner: int32 [16, 3], P('ctx'), may hold values from 0 to 7, all different within a row; in each aligned block of 2 rows (0 to 1, 2 to 3, ...) at most 2 rows name the same one
- rand_local: int32 [16, 3], P('ctx'), may hold values from 0 to 1
Outputs:
- d_queries: bfloat16 [4, 1024, 1024], P('dp', 'ctx')
- d_keys: bfloat16 [4, 1024, 1024], P('dp', 'ctx')
- d_values: bfloat16 [4, 1024, 1024], P('dp', 'ctx')
- d_glob_keys: float32 [128, 1024], replicated
- d_glob_values: float32 [128, 1024], replicated
Inputs may be any that keep to these rules, and one draw needn't show every extreme that they name: `rand_owner`: the 3 random blocks of one query block lie on different ctx indices. Among the 2 query blocks of one device no ctx index is named more than 2 times.
All inputs are finite; a program needn't handle non-finite values.
Results may differ from a plain program's by a relative error of at most 0.0055.
Values may be sent and summed in bfloat16 or wider, within the bound.
A program may use at most 128 MiB of HBM per device.

v0:
```python
import jax
import jax.numpy as jnp
from jax import lax
from jax.sharding import PartitionSpec as P

HEADS = 16
HDIM = 64
BLK = 64
GLOB = 128


def extended(block, sides, width):
    for axis, dim in sides:
        count = lax.axis_size(axis)
        forward = [(i, i + 1) for i in range(count - 1)]
        forward.append((count - 1, 0))
        backward = [(target, source) for source, target in forward]
        low = lax.ppermute(
            lax.slice_in_dim(block, block.shape[dim] - width, None, axis=dim), axis, forward
        )
        high = lax.ppermute(lax.slice_in_dim(block, 0, width, axis=dim), axis, backward)
        block = jnp.concatenate([low, block, high], axis=dim)
    return block


def block_grads(query_blk, dout_blk, lse_blk, delta_blk, key_blk, value_blk):
    scaling = HDIM ** (-0.5)
    scores = (
        jnp.einsum("nqhe,nkhe->nhqk", query_blk, key_blk, preferred_element_type=jnp.float32)
        * scaling
    )
    probability = jnp.exp(scores - lse_blk[..., None])
    prob_low = probability.astype(jnp.bfloat16)
    d_probability = jnp.einsum(
        "nqhe,nkhe->nhqk", dout_blk, value_blk, preferred_element_type=jnp.float32
    )
    d_scores = (probability * (d_probability - delta_blk[..., None])).astype(jnp.bfloat16)
    grad_q = (
        jnp.einsum("nhqk,nkhe->nqhe", d_scores, key_blk, preferred_element_type=jnp.float32)
        * scaling
    )
    grad_k = (
        jnp.einsum("nhqk,nqhe->nkhe", d_scores, query_blk, preferred_element_type=jnp.float32)
        * scaling
    )
    grad_v = jnp.einsum("nhqk,nqhe->nkhe", prob_low, dout_blk, preferred_element_type=jnp.float32)
    return (grad_q, grad_k, grad_v)


def spread_window(section):
    pad_rest = ((0, 0), (0, 0), (0, 0))
    lower = jnp.pad(section[:, :BLK], ((0, 2),) + pad_rest)
    middle = jnp.pad(section[:, BLK : 2 * BLK], ((1, 1),) + pad_rest)
    upper = jnp.pad(section[:, 2 * BLK :], ((2, 0),) + pad_rest)
    return lower + middle + upper


def shards(
    queries, keys, values, outputs, d_out, lse, glob_keys, glob_values, rand_owner, rand_local
):
    tokens_dev = queries.shape[1]
    feature_dim = queries.shape[2]
    blocks = tokens_dev // BLK
    cycle_size = lax.axis_size("ctx")
    per_block = rand_owner.shape[1]
    pairs = blocks * per_block
    query_blk = queries.reshape(blocks, BLK, HEADS, HDIM)
    dout_blk = d_out.reshape(blocks, BLK, HEADS, HDIM)
    product = d_out.astype(jnp.float32) * outputs.astype(jnp.float32)
    delta_blk = jnp.sum(product.reshape(blocks, BLK, HEADS, HDIM), axis=3).transpose(0, 2, 1)
    lse_blk = lse.reshape(HEADS, blocks, BLK).transpose(1, 0, 2)
    key_value = jnp.stack([keys[0], values[0]])
    padded = extended(key_value, (("ctx", 1),), BLK)

    def split_blocks(section):
        return section.reshape(2, blocks, BLK, HEADS, HDIM)

    window = jnp.concatenate(
        [
            split_blocks(padded[:, :tokens_dev]),
            split_blocks(padded[:, BLK : BLK + tokens_dev]),
            split_blocks(padded[:, 2 * BLK :]),
        ],
        axis=2,
    )
    dq_win, dk_win, dv_win = block_grads(
        query_blk, dout_blk, lse_blk, delta_blk, window[0], window[1]
    )
    grad_grid = jnp.stack([spread_window(dk_win), spread_window(dv_win)]).reshape(
        2, tokens_dev + 2 * BLK, feature_dim
    )
    edge_rims = jnp.concatenate([grad_grid[:, :BLK], grad_grid[:, tokens_dev + BLK :]], axis=1)
    returned = extended(edge_rims, (("ctx", 1),), BLK)
    kv_grad = grad_grid[:, BLK : tokens_dev + BLK]
    kv_grad = kv_grad.at[:, :BLK].add(returned[:, :BLK])
    kv_grad = kv_grad.at[:, tokens_dev - BLK :].add(returned[:, 3 * BLK :])
    mem_keys = jnp.broadcast_to(
        glob_keys.reshape(1, GLOB, HEADS, HDIM), (blocks, GLOB, HEADS, HDIM)
    )
    mem_values = jnp.broadcast_to(
        glob_values.reshape(1, GLOB, HEADS, HDIM), (blocks, GLOB, HEADS, HDIM)
    )
    dq_mem, dk_mem, dv_mem = block_grads(
        query_blk, dout_blk, lse_blk, delta_blk, mem_keys, mem_values
    )
    mem_terms = jnp.stack([jnp.sum(dk_mem, axis=0), jnp.sum(dv_mem, axis=0)]).reshape(
        2, GLOB, feature_dim
    )
    memory_total = lax.psum(mem_terms, ("dp", "ctx"))
    capacity = min(blocks, max(2, 2 * blocks * per_block // cycle_size))
    owner_flat = rand_owner.reshape(-1)
    local_flat = rand_local.reshape(-1)
    owner_hits = (owner_flat[:, None] == jnp.arange(cycle_size, dtype=jnp.int32)[None, :]).astype(
        jnp.int32
    )
    earlier = jnp.cumsum(owner_hits, axis=0) - owner_hits
    slot_rank = jnp.sum(earlier * owner_hits, axis=1)
    slot_index = owner_flat * capacity + slot_rank
    wanted = (
        jnp.zeros((cycle_size * capacity,), jnp.int32)
        .at[slot_index]
        .set(local_flat)
        .reshape(cycle_size, capacity)
    )
    kv_blocks = jnp.stack(
        [keys[0].reshape(blocks, BLK, feature_dim), values[0].reshape(blocks, BLK, feature_dim)],
        axis=1,
    )
    query_pairs = jnp.repeat(query_blk, per_block, axis=0)
    dout_pairs = jnp.repeat(dout_blk, per_block, axis=0)
    lse_pairs = jnp.repeat(lse_blk, per_block, axis=0)
    delta_pairs = jnp.repeat(delta_blk, per_block, axis=0)
    slots_all = cycle_size * capacity
    asked_ids = lax.all_to_all(wanted, "ctx", split_axis=0, concat_axis=0, tiled=True)
    picked = kv_blocks[asked_ids]
    fetched, asked_ids = (
        lax.all_to_all(picked, "ctx", split_axis=0, concat_axis=0, tiled=True),
        asked_ids,
    )
    chosen = fetched.reshape(slots_all, 2, BLK, HEADS, HDIM)[slot_index]
    dq_pair, dk_pair, dv_pair = block_grads(
        query_pairs, dout_pairs, lse_pairs, delta_pairs, chosen[:, 0], chosen[:, 1]
    )
    dq_rand = lax.optimization_barrier(dq_pair.astype(jnp.bfloat16)).astype(jnp.float32)
    pair_grads = (
        jnp.stack([dk_pair, dv_pair], axis=1)
        .reshape(pairs, 2, BLK, feature_dim)
        .astype(jnp.bfloat16)
    )
    grad_slots = (
        jnp.zeros((slots_all, 2, BLK, feature_dim), jnp.bfloat16).at[slot_index].set(pair_grads)
    )
    arrived = lax.all_to_all(
        grad_slots.reshape(cycle_size, capacity, 2, BLK, feature_dim),
        "ctx",
        split_axis=0,
        concat_axis=0,
        tiled=True,
    )
    received = arrived.reshape(slots_all, 2, BLK, feature_dim)
    kv_rand = (
        jnp.zeros((blocks, 2, BLK, feature_dim), jnp.float32)
        .at[asked_ids.reshape(-1)]
        .add(received.astype(jnp.float32))
    )
    dq_rand_sum = jnp.sum(dq_rand.reshape(blocks, per_block, BLK, HEADS, HDIM), axis=1)
    grad_queries = (
        (dq_win + dq_mem + dq_rand_sum).reshape(1, tokens_dev, feature_dim).astype(jnp.bfloat16)
    )
    grad_keys = (
        (kv_grad[0] + kv_rand[:, 0].reshape(tokens_dev, feature_dim))
        .reshape(1, tokens_dev, feature_dim)
        .astype(jnp.bfloat16)
    )
    grad_values = (
        (kv_grad[1] + kv_rand[:, 1].reshape(tokens_dev, feature_dim))
        .reshape(1, tokens_dev, feature_dim)
        .astype(jnp.bfloat16)
    )
    return (grad_queries, grad_keys, grad_values, memory_total[0], memory_total[1])


def solution(mesh):
    return jax.shard_map(
        shards,
        mesh=mesh,
        in_specs=(
            P("dp", "ctx", None),
            P("dp", "ctx", None),
            P("dp", "ctx", None),
            P("dp", "ctx", None),
            P("dp", "ctx", None),
            P("dp", None, "ctx"),
            P(),
            P(),
            P("ctx", None),
            P("ctx", None),
        ),
        out_specs=(P("dp", "ctx", None), P("dp", "ctx", None), P("dp", "ctx", None), P(), P()),
        check_vma=False,
    )
```

profile of v0, /device:TPU:0, one launch (start us, length us, event | category | flops | bytes accessed | tf_op | source)
XLA Modules:
  0.0 246.8 jit_solution(17565777443147992249)
XLA Ops:
  11.0 5.2 %all-to-all-start = ((s32[8,1,2]{2,1,0:T(1,128)}), s32[8,1,2]{2,1,0:T(1,128)S(1)}, u32[]{:S(2)}, u32[]{:S(2)}) async-start(s32[8,1,2]{2,1,0:T(1,128)} %bitcast.12), calls=%async_computation | async-start | bytes 8192 | tf_op jit(solution)/shard_map/all_to_all | solution.py:134
  17.3 3.5 %all-to-all-done = s32[8,1,2]{2,1,0:T(1,128)S(1)} async-done(((s32[8,1,2]{2,1,0:T(1,128)}), s32[8,1,2]{2,1,0:T(1,128)S(1)}, u32[]{:S(2)}, u32[]{:S(2)}) %all-to-all-start) | async-done | bytes 96 | tf_op jit(solution)/shard_map/all_to_all | solution.py:134
  21.0 2.8 %gather_fusion = bf16[16,2,64,1024]{3,2,1,0:T(8,128)(2,1)} fusion(bf16[2,2,64,1024]{3,2,0,1:T(8,128)(2,1)S(1)} %pad_maximum_fusion.5, s32[1024]{0:T(1024)S(1)} %pad_clamp_fusion.1), kind=kCustom, calls=%fused_computation | custom fusion | bytes 8388672 | tf_op jit(solution)/shard_map/gather | solution.py:135
  23.8 4.7 %all-to-all-start.1 = ((bf16[8,2,2,64,1024]{4,3,2,1,0:T(8,128)(2,1)}), bf16[8,2,2,64,1024]{4,3,2,1,0:T(8,128)(2,1)}, u32[]{:S(2)}, u32[]{:S(2)}) async-start(bf16[8,2,2,64,1024]{4,3,2,1,0:T(8,128)(2,1)} %bitcast.105), calls=%async_computation.1 | async-start | bytes 8388608 | tf_op jit(solution)/shard_map/all_to_all | solution.py:137
  29.9 2.3 collective-permute-start.1
  42.5 2.0 copy.129
  45.7 39.9 %collective-permute-done = bf16[2,64,1024]{2,1,0:T(8,128)(2,1)} collective-permute-done((bf16[2,64,1024]{2,1,0:T(8,128)(2,1)}, bf16[2,64,1024]{2,1,0:T(8,128)(2,1)}, u32[]{:S(2)}, u32[]{:S(2)}) %collective-permute-start) | collective-permute-done | bytes 262176 | tf_op jit(solution)/shard_map/ppermute | solution.py:18
  87.5 2.5 %reshape.256 = bf16[2,2,64,16,64]{4,3,2,1,0:T(8,128)(2,1)} reshape(bf16[2,128,1024]{2,1,0:T(8,128)(2,1)} %get-tuple-element.66) | data formatting | bytes 1048576 | tf_op jit(solution)/shard_map/reshape | solution.py:76
  90.0 2.7 %copy.130 = bf16[2,2,64,16,64]{2,4,3,1,0:T(8,128)(2,1)} copy(bf16[2,2,64,16,64]{4,3,2,1,0:T(8,128)(2,1)} %reshape.256) | data formatting | bytes 1048576 | tf_op jit(solution)/shard_map/reshape | solution.py:76
  94.3 2.7 %copy.128 = bf16[2,2,64,16,64]{2,4,3,1,0:T(8,128)(2,1)} copy(bf16[2,2,64,16,64]{4,3,2,1,0:T(8,128)(2,1)} %reshape.254) | data formatting | bytes 1048576 | tf_op jit(solution)/shard_map/reshape | solution.py:76
  97.0 2.5 %pad_maximum_fusion = bf16[2,2,192,16,64]{2,4,3,1,0:T(8,128)(2,1)S(1)} fusion(bf16[2,2,64,16,64]{2,4,3,1,0:T(8,128)(2,1)} %copy.130, bf16[2,2,64,16,64]{2,4,3,1,0:T(8,128)(2,1)S(1)} %copy.129, bf16[2,2,64,16,64]{2,4,3,1,0:T(8,128)(2,1)} %copy.128), kind=kLoop, calls=%fused_computation.12 | loop fusion | flops 4718592 | bytes 3145728 | tf_op jit(solution)/shard_map/concatenate | solution.py:78
  104.3 11.6 %reshape.262 = bf16[16,2,64,16,64]{4,3,2,1,0:T(8,128)(2,1)} reshape(bf16[8,2,2,64,1024]{4,3,2,1,0:T(8,128)(2,1)} %all-to-all-done.1) | data formatting | bytes 8388608 | tf_op jit(solution)/shard_map/reshape | solution.py:140
  115.9 4.5 %gather_fusion.1 = bf16[6,2,64,16,64]{4,3,2,1,0:T(8,128)(2,1)S(1)} fusion(bf16[16,2,64,16,64]{4,3,2,1,0:T(8,128)(2,1)} %reshape.262, s32[1024]{0:T(1024)S(1)} %pad_clamp_fusion), kind=kCustom, calls=%fused_computation.1 | custom fusion | bytes 3145752 | tf_op jit(solution)/shard_map/gather | solution.py:140
  125.7 2.2 copy.156
  127.9 3.4 %stack.39 = bf16[6,1,64,1024]{3,2,0,1:T(8,128)(2,1)} reshape(bf16[6,64,16,64]{3,2,1,0:T(8,128)(2,1)} %copy.156) | data formatting | bytes 1572864 | tf_op jit(solution)/shard_map/stack | solution.py:146
  131.4 3.1 %multiply_convert_fusion.2 = bf16[6,16,64,64]{3,2,1,0:T(8,128)(2,1)S(1)} fusion(f32[6,16,64,64]{3,2,1,0:T(8,128)S(1)} %fusion.10, bf16[6,64,16,64]{3,1,2,0:T(8,128)(2,1)} %bitcast.109, bf16[6,1,64,16,64]{4,3,2,1,0:T(8,128)(2,1)} %get-tuple-element.49, f32[6,16,64]{2,1,0:T(8,128)S(1)} %bitcast.127, f32[6,16,64]{2,1,0:T(8,128)S(1)} %bitcast.121), kind=kOutput, calls=%fused_computation.9 | convolution fusion | flops 52297728 | bytes 3981312 | tf_op jit(solution)/shard_map/nqhe,nkhe->nhqk/dot_general | solution.py:34
  138.1 2.5 %broadcast_in_dim.51 = bf16[16,2,64,1024]{3,2,1,0:T(8,128)(2,1)} broadcast(bf16[]{:T(256)} %constant.82.clone.1), dimensions={} | broadcast | bytes 4194306 | tf_op jit(solution)/shard_map/broadcast_in_dim | solution.py:151
  140.6 4.8 %scatter_fusion = bf16[16,2,64,1024]{3,2,1,0:T(8,128)(2,1)} fusion(bf16[16,2,64,1024]{3,2,1,0:T(8,128)(2,1)} %broadcast_in_dim.51, s32[6]{0:T(128)S(1)} %fusion.34, bf16[6,2,64,1024]{3,2,1,0:T(8,128)(2,1)S(1)} %copy.157), kind=kCustom, calls=%fused_computation.3 | custom fusion | bytes 4718616 | tf_op jit(solution)/shard_map/scatter | solution.py:151
  145.4 5.0 %all-to-all-start.2 = ((bf16[8,2,2,64,1024]{4,3,2,1,0:T(8,128)(2,1)}), bf16[8,2,2,64,1024]{4,3,2,1,0:T(8,128)(2,1)}, u32[]{:S(2)}, u32[]{:S(2)}) async-start(bf16[8,2,2,64,1024]{4,3,2,1,0:T(8,128)(2,1)} %bitcast.104), calls=%async_computation.2 | async-start | bytes 8388608 | tf_op jit(solution)/shard_map/all_to_all | solution.py:153
  151.3 2.0 copy.152
  153.3 2.9 %stack.35 = f32[1,256,1024]{2,1,0:T(8,128)} reshape(f32[4,64,16,64]{3,2,1,0:T(8,128)} %copy.152) | data formatting | bytes 2097152 | tf_op jit(solution)/shard_map/stack | solution.py:89
  158.1 2.0 copy.154
  160.2 2.1 stack.36
  164.8 2.5 %collective-permute-start.3 = (f32[2,64,1024]{2,1,0:T(8,128)}, f32[2,64,1024]{2,1,0:T(8,128)}, u32[]{:S(2)}, u32[]{:S(2)}) collective-permute-start(f32[2,64,1024]{2,1,0:T(8,128)} %get-tuple-element.51), channel_id=1, source_target_pairs={{1,0},{2,1},{3,2},{4,3},{5,4},{6,5},{7,6},{0,7},{9,8},{10,9},{11,1... | collective-permute-start | bytes 1572872 | tf_op jit(solution)/shard_map/ppermute | solution.py:21
  168.8 10.2 %all-reduce.8.cloned.1.call-done = f32[2,128,1024]{1,2,0:T(8,128)} async-done(((f32[2,128,1024]{1,2,0:T(8,128)}), f32[2,128,1024]{1,2,0:T(8,128)}) %all-reduce.8.cloned.1.call-update) | async-done | bytes 1048592 | tf_op jit(solution)/shard_map/psum | solution.py:109
  179.0 2.1 slice_bitcast_fusion.5
  182.1 2.2 copy.161
  184.3 27.9 %collective-permute-done.2 = f32[2,64,1024]{2,1,0:T(8,128)} collective-permute-done((f32[2,64,1024]{2,1,0:T(8,128)}, f32[2,64,1024]{2,1,0:T(8,128)}, u32[]{:S(2)}, u32[]{:S(2)}) %collective-permute-start.2) | collective-permute-done | bytes 524320 | tf_op jit(solution)/shard_map/ppermute | solution.py:18
  212.2 2.1 fusion.27
  214.3 2.1 fusion.26
  220.4 6.5 %bitcast_convert_fusion = f32[16,2,64,1024]{3,2,1,0:T(8,128)} fusion(bf16[8,2,2,64,1024]{4,3,2,1,0:T(8,128)(2,1)} %all-to-all-done.2), kind=kLoop, calls=%fused_computation.5 | loop fusion | flops 2097152 | bytes 12582912 | tf_op jit(solution)/shard_map/convert_element_type | solution.py:164
  227.1 10.8 %scatter_fusion.1 = f32[2,2,64,1024]{3,2,1,0:T(8,128)S(1)} fusion(f32[2,2,64,1024]{3,2,1,0:T(8,128)S(1)} %broadcast_in_dim.50, s32[16]{0:T(128)S(1)} %fusion.35, f32[16,2,64,1024]{3,2,1,0:T(8,128)} %bitcast_convert_fusion), kind=kCustom, calls=%fused_computation.4 | custom fusion | flops 2097152 | bytes 25165888 | tf_op jit(solution)/shard_map/scatter-add | solution.py:164
  (148 shorter events, 48.9 us)
Async XLA Ops:
  11.0 9.8 %all-to-all-start = ((s32[8,1,2]{2,1,0:T(1,128)}), s32[8,1,2]{2,1,0:T(1,128)S(1)}, u32[]{:S(2)}, u32[]{:S(2)}) async-start(s32[8,1,2]{2,1,0:T(1,128)} %bitcast.12), calls=%async_computation | async-start | bytes 8192 | tf_op jit(solution)/shard_map/all_to_all | solution.py:134
  23.8 4.8 %copy-start.26 = (bf16[1,128,1024]{2,1,0:T(8,128)(2,1)S(1)}, bf16[1,128,1024]{2,1,0:T(8,128)(2,1)}, u32[]{:S(2)}) copy-start(bf16[1,128,1024]{2,1,0:T(8,128)(2,1)} %param.15) | copy-start | bytes 786436
  23.8 4.9 %copy-start.27 = (bf16[1,128,1024]{2,1,0:T(8,128)(2,1)S(1)}, bf16[1,128,1024]{2,1,0:T(8,128)(2,1)}, u32[]{:S(2)}) copy-start(bf16[1,128,1024]{2,1,0:T(8,128)(2,1)} %param.16) | copy-start | bytes 786436
  23.8 80.5 %all-to-all-start.1 = ((bf16[8,2,2,64,1024]{4,3,2,1,0:T(8,128)(2,1)}), bf16[8,2,2,64,1024]{4,3,2,1,0:T(8,128)(2,1)}, u32[]{:S(2)}, u32[]{:S(2)}) async-start(bf16[8,2,2,64,1024]{4,3,2,1,0:T(8,128)(2,1)} %bitcast.105), calls=%async_computation.1 | async-start | bytes 8388608 | tf_op jit(solution)/shard_map/all_to_all | solution.py:137
  28.5 3.6 %copy-start.28 = (bf16[1,128,1024]{2,1,0:T(8,128)(2,1)S(1)}, bf16[1,128,1024]{2,1,0:T(8,128)(2,1)}, u32[]{:S(2)}) copy-start(bf16[1,128,1024]{2,1,0:T(8,128)(2,1)} %param.14) | copy-start | bytes 786436
  28.6 4.0 %copy-start.25 = (bf16[1,128,1024]{2,1,0:T(8,128)(2,1)S(1)}, bf16[1,128,1024]{2,1,0:T(8,128)(2,1)}, u32[]{:S(2)}) copy-start(bf16[1,128,1024]{2,1,0:T(8,128)(2,1)} %param.18) | copy-start | bytes 786436
  28.6 4.3 %copy-start.29 = (bf16[1,128,1024]{2,1,0:T(8,128)(2,1)S(1)}, bf16[1,128,1024]{2,1,0:T(8,128)(2,1)}, u32[]{:S(2)}) copy-start(bf16[1,128,1024]{2,1,0:T(8,128)(2,1)} %param.17) | copy-start | bytes 786436
  28.6 150.4 %all-reduce.8.cloned.1.call-start = ((), (), s32[]{:S(2)}) async-start(), calls=%async_computation.3 | async-start | bytes 2097152 | tf_op jit(solution)/shard_map/psum | solution.py:109
  29.5 56.1 %collective-permute-start = (bf16[2,64,1024]{2,1,0:T(8,128)(2,1)}, bf16[2,64,1024]{2,1,0:T(8,128)(2,1)}, u32[]{:S(2)}, u32[]{:S(2)}) collective-permute-start(bf16[2,64,1024]{2,1,0:T(8,128)(2,1)} %get-tuple-element.67), channel_id=1, source_target_pairs={{0,1},{1,2},{2,3},{3,4},{4,5},{5,6},{6,7},{7,0},{8,9},{9,10},{10,1... | collective-permute-start | bytes 786440 | tf_op jit(solution)/shard_map/ppermute | solution.py:18
  29.9 55.7 %collective-permute-start.1 = (bf16[2,64,1024]{2,1,0:T(8,128)(2,1)}, bf16[2,64,1024]{2,1,0:T(8,128)(2,1)}, u32[]{:S(2)}, u32[]{:S(2)}) collective-permute-start(bf16[2,64,1024]{2,1,0:T(8,128)(2,1)} %get-tuple-element.68), channel_id=1, source_target_pairs={{1,0},{2,1},{3,2},{4,3},{5,4},{6,5},{7,6},{0,7},{9,8},{10,9},{11,1... | collective-permute-start | bytes 786440 | tf_op jit(solution)/shard_map/ppermute | solution.py:21
  32.9 67.1 %copy-start.2 = (bf16[2,64,16,64]{3,2,1,0:T(8,128)(2,1)}, bf16[2,64,16,64]{3,2,1,0:T(8,128)(2,1)S(1)}, u32[]{:S(2)}) copy-start(bf16[2,64,16,64]{3,2,1,0:T(8,128)(2,1)S(1)} %reshape.259) | copy-start | bytes 786436
  99.6 1.3 copy-start.11
  100.0 1.5 copy-start
  120.5 1.8 copy-start.24
  122.3 1.4 copy-start.4
  122.7 1.3 copy-start.6
  122.7 1.4 copy-start.23
  131.4 3.1 %copy-start.7 = (bf16[2,3,64,16,64]{4,2,3,1,0:T(8,128)(2,1)S(1)}, bf16[2,3,64,16,64]{4,2,3,1,0:T(8,128)(2,1)}, u32[]{:S(2)}) copy-start(bf16[2,3,64,16,64]{4,2,3,1,0:T(8,128)(2,1)} %copy-done.6) | copy-start | bytes 2359300
  135.6 2.2 copy-start.22
  145.4 5.0 %copy-start.13 = (f32[2,192,16,64]{1,3,2,0:T(8,128)S(1)}, f32[2,192,16,64]{1,3,2,0:T(8,128)}, u32[]{:S(2)}) copy-start(f32[2,192,16,64]{1,3,2,0:T(8,128)} %multiply_bitcast_fusion) | copy-start | bytes 4718596
  145.4 75.0 %all-to-all-start.2 = ((bf16[8,2,2,64,1024]{4,3,2,1,0:T(8,128)(2,1)}), bf16[8,2,2,64,1024]{4,3,2,1,0:T(8,128)(2,1)}, u32[]{:S(2)}, u32[]{:S(2)}) async-start(bf16[8,2,2,64,1024]{4,3,2,1,0:T(8,128)(2,1)} %bitcast.104), calls=%async_computation.2 | async-start | bytes 8388608 | tf_op jit(solution)/shard_map/all_to_all | solution.py:153
  153.3 2.9 %copy-start.1 = (f32[2,16,192,64]{2,3,1,0:T(8,128)S(1)}, f32[2,16,192,64]{2,3,1,0:T(8,128)}, u32[]{:S(2)}) copy-start(f32[2,16,192,64]{2,3,1,0:T(8,128)} %copy-done) | copy-start | bytes 4718596
  153.3 2.9 %copy-start.3 = (bf16[2,64,16,64]{3,2,1,0:T(8,128)(2,1)S(1)}, bf16[2,64,16,64]{3,2,1,0:T(8,128)(2,1)}, u32[]{:S(2)}) copy-start(bf16[2,64,16,64]{3,2,1,0:T(8,128)(2,1)} %copy-done.2) | copy-start | bytes 786436
  160.2 2.1 copy-start.21
  162.4 2.2 copy-start.17
  162.4 4.9 %copy-start.12 = (bf16[2,2,192,16,64]{2,4,3,1,0:T(8,128)(2,1)S(1)}, bf16[2,2,192,16,64]{2,4,3,1,0:T(8,128)(2,1)}, u32[]{:S(2)}) copy-start(bf16[2,2,192,16,64]{2,4,3,1,0:T(8,128)(2,1)} %copy-done.11) | copy-start | bytes 4718596
  162.4 4.9 %copy-start.15 = (bf16[2,16,192,64]{2,3,1,0:T(8,128)(2,1)S(1)}, bf16[2,16,192,64]{2,3,1,0:T(8,128)(2,1)}, u32[]{:S(2)}) copy-start(bf16[2,16,192,64]{2,3,1,0:T(8,128)(2,1)} %copy-done.14) | copy-start | bytes 2359300
  164.7 47.5 %collective-permute-start.2 = (f32[2,64,1024]{2,1,0:T(8,128)}, f32[2,64,1024]{2,1,0:T(8,128)}, u32[]{:S(2)}, u32[]{:S(2)}) collective-permute-start(f32[2,64,1024]{2,1,0:T(8,128)} %get-tuple-element.52), channel_id=1, source_target_pairs={{0,1},{1,2},{2,3},{3,4},{4,5},{5,6},{6,7},{7,0},{8,9},{9,10},{10,1... | collective-permute-start | bytes 1572872 | tf_op jit(solution)/shard_map/ppermute | solution.py:18
  164.8 49.4 %collective-permute-start.3 = (f32[2,64,1024]{2,1,0:T(8,128)}, f32[2,64,1024]{2,1,0:T(8,128)}, u32[]{:S(2)}, u32[]{:S(2)}) collective-permute-start(f32[2,64,1024]{2,1,0:T(8,128)} %get-tuple-element.51), channel_id=1, source_target_pairs={{1,0},{2,1},{3,2},{4,3},{5,4},{6,5},{7,6},{0,7},{9,8},{10,9},{11,1... | collective-permute-start | bytes 1572872 | tf_op jit(solution)/shard_map/ppermute | solution.py:21
  182.1 34.3 %copy-start.5 = (bf16[6,1,64,16,64]{4,3,2,1,0:T(8,128)(2,1)S(1)}, bf16[6,1,64,16,64]{4,3,2,1,0:T(8,128)(2,1)}, u32[]{:S(2)}) copy-start(bf16[6,1,64,16,64]{4,3,2,1,0:T(8,128)(2,1)} %copy-done.4) | copy-start | bytes 2359300
  182.1 34.3 %copy-start.9 = (bf16[6,16,64,64]{3,2,1,0:T(8,128)(2,1)S(1)}, bf16[6,16,64,64]{3,2,1,0:T(8,128)(2,1)}, u32[]{:S(2)}) copy-start(bf16[6,16,64,64]{3,2,1,0:T(8,128)(2,1)} %copy-done.8) | copy-start | bytes 2359300
  217.1 1.4 copy-start.20
  (7 other events, 7.2 us)
Sparse Core Ops, SparseCore 0:
  39.0 139.9 all-reduce.7
where the time goes:
time: 248 us; the launch traced here: 247 us
  local copies, waits for them, and re-layouts  84.7 us (34%)
  waiting for transfers between devices  81.6 us (33%)
  other arithmetic  32.2 us (13%)
  starting transfers between devices  20.2 us (8%)
  between operations  14.7 us (6%)
  matrix products  13.6 us (5%)
    ppermute x2, waiting for transfers between devices, extended(): lax.ppermute(lax.slice_in_dim(block, block.shape[dim] - width, None, axis...  67.8 us
    reshape x6, local copies, waits for them, and re-layouts, split_blocks(): return section.reshape(2, blocks, BLK, HEADS, HDIM)  13.2 us
    reshape x1, local copies, waits for them, and re-layouts, shards(): chosen = fetched.reshape(slots_all, 2, BLK, HEADS, HDIM)[slot_index]  11.6 us
    unnamed x68, local copies, waits for them, and re-layouts  11.1 us
    scatter-add x1, other arithmetic, shards(): kv_rand = jnp.zeros((blocks, 2, BLK, feature_dim), jnp.float32).at[asked_...  10.8 us
    psum x1, waiting for transfers between devices, shards(): memory_total = lax.psum(mem_terms, ('dp', 'ctx'))  10.2 us
    convert_element_type x1, other arithmetic, shards(): received.astype(jnp.float32)  6.53 us
    all_to_all x1, starting transfers between devices, shards(): lax.all_to_all(wanted, 'ctx', split_axis=0, concat_axis=0, tiled=True)  5.17 us
  transfers between devices with their start and end apart: 8, of which 4 were waited for; matrix products, arithmetic and copies ran while one was open for 40% of the time, Pallas kernels for 0%

commit v1 on v0

--- a/solution.py
+++ b/solution.py
@@ -7,6 +7,11 @@
 HDIM = 64
 BLK = 64
 GLOB = 128
+
+
+def gather_and_add(array, axis):
+    terms = lax.all_gather(array, axis)
+    return jnp.sum(terms, axis=0)
 
 
 def extended(block, sides, width):
@@ -106,7 +111,7 @@
     mem_terms = jnp.stack([jnp.sum(dk_mem, axis=0), jnp.sum(dv_mem, axis=0)]).reshape(
         2, GLOB, feature_dim
     )
-    memory_total = lax.psum(mem_terms, ("dp", "ctx"))
+    memory_total = gather_and_add(mem_terms, ("dp", "ctx"))
     capacity = min(blocks, max(2, 2 * blocks * per_block // cycle_size))
     owner_flat = rand_owner.reshape(-1)
     local_flat = rand_local.reshape(-1)

time: 248 us -> 306 us (1.23)
  waiting for transfers between devices: 81.6 us -> 142 us
  local copies, waits for them, and re-layouts: 84.7 us -> 76.8 us
  other arithmetic: 32.2 us -> 39 us
    ppermute x2, waiting for transfers between devices: 67.8 us -> 138 us  [extended(): lax.ppermute(lax.slice_in_dim(block, block.shape[dim] - width, None, axis...]
    reduce_sum x0 -> x1, other arithmetic: none -> 11.9 us  [gather_and_add(): return jnp.sum(terms, axis=0)]
    psum x1 -> x0, waiting for transfers between devices: 10.2 us -> none  [shards(): memory_total = lax.psum(mem_terms, ('dp', 'ctx'))]
    unnamed x68 -> x56, local copies, waits for them, and re-layouts: 11.1 us -> 4.98 us
  transfers between devices with their start and end apart: 8 -> 8, of which waited for: 4 -> 3; matrix products, arithmetic and copies ran while one was open for 40% -> 33% of each run, Pallas kernels for 0% -> 0%
where the time goes in v1:
time: 306 us; the launch traced here: 305 us
  waiting for transfers between devices  142 us (46%)
  local copies, waits for them, and re-layouts  76.8 us (25%)
  other arithmetic  39 us (13%)
  starting transfers between devices  19.9 us (7%)
  between operations  14.8 us (5%)
  matrix products  12 us (4%)
    ppermute x2, waiting for transfers between devices, extended(): lax.ppermute(lax.slice_in_dim(block, block.shape[dim] - width, None, axis...  138 us
    reshape x6, local copies, waits for them, and re-layouts, split_blocks(): return section.reshape(2, blocks, BLK, HEADS, HDIM)  13.1 us
    reshape x1, local copies, waits for them, and re-layouts, shards(): chosen = fetched.reshape(slots_all, 2, BLK, HEADS, HDIM)[slot_index]  11.9 us
    reduce_sum x1, other arithmetic, gather_and_add(): return jnp.sum(terms, axis=0)  11.9 us
    scatter-add x1, other arithmetic, shards(): kv_rand = jnp.zeros((blocks, 2, BLK, feature_dim), jnp.float32).at[asked_...  10.8 us
    convert_element_type x1, other arithmetic, shards(): received.astype(jnp.float32)  7.11 us
  transfers between devices with their start and end apart: 8, of which 3 were waited for; matrix products, arithmetic and copies ran while one was open for 33% of the time, Pallas kernels for 0%

profile of v1, /device:TPU:0, one launch (start us, length us, event | category | flops | bytes accessed | tf_op | source)
XLA Modules:
  0.0 304.7 jit_solution(18110211301348074340)
XLA Ops:
  18.8 5.2 %all-to-all-start = ((s32[8,1,2]{2,1,0:T(1,128)}), s32[8,1,2]{2,1,0:T(1,128)S(1)}, u32[]{:S(2)}, u32[]{:S(2)}) async-start(s32[8,1,2]{2,1,0:T(1,128)} %bitcast.12), calls=%async_computation | async-start | bytes 8192 | tf_op jit(solution)/shard_map/all_to_all | solution.py:139
  24.0 4.5 %all-to-all-done = s32[8,1,2]{2,1,0:T(1,128)S(1)} async-done(((s32[8,1,2]{2,1,0:T(1,128)}), s32[8,1,2]{2,1,0:T(1,128)S(1)}, u32[]{:S(2)}, u32[]{:S(2)}) %all-to-all-start) | async-done | bytes 96 | tf_op jit(solution)/shard_map/all_to_all | solution.py:139
  28.8 2.8 gather_fusion
  31.6 4.5 %all-to-all-start.1 = ((bf16[8,2,2,64,1024]{4,3,2,1,0:T(8,128)(2,1)}), bf16[8,2,2,64,1024]{4,3,2,1,0:T(8,128)(2,1)}, u32[]{:S(2)}, u32[]{:S(2)}) async-start(bf16[8,2,2,64,1024]{4,3,2,1,0:T(8,128)(2,1)} %bitcast.107), calls=%async_computation.1 | async-start | bytes 8388608 | tf_op jit(solution)/shard_map/all_to_all | solution.py:142
  36.7 2.3 collective-permute-start.1
  38.9 1.6 reshape.254
  42.4 2.0 copy.162
  45.7 71.5 %collective-permute-done = bf16[2,64,1024]{2,1,0:T(8,128)(2,1)} collective-permute-done((bf16[2,64,1024]{2,1,0:T(8,128)(2,1)S(1)}, bf16[2,64,1024]{2,1,0:T(8,128)(2,1)}, u32[]{:S(2)}, u32[]{:S(2)}) %collective-permute-start) | collective-permute-done | bytes 262176 | tf_op jit(solution)/shard_map/ppermute | solution.py:23
  117.2 1.9 pad_maximum_fusion.4
  119.2 2.5 reshape.253
  121.6 2.7 copy.161
  124.3 1.6 reshape.255
  126.0 2.7 copy.163
  128.6 2.5 pad_maximum_fusion
  134.2 1.8 multiply_bitcast_fusion
  136.0 11.9 %reshape.261 = bf16[16,2,64,16,64]{4,3,2,1,0:T(8,128)(2,1)} reshape(bf16[8,2,2,64,1024]{4,3,2,1,0:T(8,128)(2,1)} %all-to-all-done.1) | data formatting | bytes 8388608 | tf_op jit(solution)/shard_map/reshape | solution.py:145
  147.9 4.8 %gather_fusion.1 = bf16[6,2,64,16,64]{4,3,2,1,0:T(8,128)(2,1)S(1)} fusion(bf16[16,2,64,16,64]{4,3,2,1,0:T(8,128)(2,1)} %reshape.261, s32[1024]{0:T(1024)S(1)} %pad_clamp_fusion), kind=kCustom, calls=%fused_computation.1 | custom fusion | bytes 3145752 | tf_op jit(solution)/shard_map/gather | solution.py:145
  157.9 2.2 copy.188
  160.1 3.5 %stack.38 = bf16[6,1,64,1024]{3,2,0,1:T(8,128)(2,1)} reshape(bf16[6,64,16,64]{3,2,1,0:T(8,128)(2,1)} %copy.188) | data formatting | bytes 1572864 | tf_op jit(solution)/shard_map/stack | solution.py:151
  163.6 2.1 fusion.5
  168.2 2.5 broadcast_in_dim.51
  170.7 4.8 %scatter_fusion = bf16[16,2,64,1024]{3,2,1,0:T(8,128)(2,1)} fusion(bf16[16,2,64,1024]{3,2,1,0:T(8,128)(2,1)} %broadcast_in_dim.51, s32[6]{0:T(128)S(1)} %fusion.34, bf16[6,2,64,1024]{3,2,1,0:T(8,128)(2,1)S(1)} %copy.190), kind=kCustom, calls=%fused_computation.3 | custom fusion | bytes 4718616 | tf_op jit(solution)/shard_map/scatter | solution.py:156
  175.5 4.7 %all-to-all-start.2 = ((bf16[8,2,2,64,1024]{4,3,2,1,0:T(8,128)(2,1)}), bf16[8,2,2,64,1024]{4,3,2,1,0:T(8,128)(2,1)}, u32[]{:S(2)}, u32[]{:S(2)}) async-start(bf16[8,2,2,64,1024]{4,3,2,1,0:T(8,128)(2,1)} %bitcast.106), calls=%async_computation.2 | async-start | bytes 8388608 | tf_op jit(solution)/shard_map/all_to_all | solution.py:158
  181.2 2.0 copy.185
  183.2 2.9 stack.35
  188.0 2.0 copy.187
  190.0 2.1 stack.36
  193.0 2.3 collective-permute-start.3
  195.7 66.2 %collective-permute-done.2 = f32[2,64,1024]{2,1,0:T(8,128)S(1)} collective-permute-done((f32[2,64,1024]{2,1,0:T(8,128)S(1)}, f32[2,64,1024]{2,1,0:T(8,128)S(1)}, u32[]{:S(2)}, u32[]{:S(2)}) %collective-permute-start.2) | collective-permute-done | bytes 524320 | tf_op jit(solution)/shard_map/ppermute | solution.py:23
  265.9 7.1 %bitcast_convert_fusion = f32[16,2,64,1024]{3,2,1,0:T(8,128)} fusion(bf16[8,2,2,64,1024]{4,3,2,1,0:T(8,128)(2,1)} %all-to-all-done.2), kind=kLoop, calls=%fused_computation.5 | loop fusion | flops 2097152 | bytes 12582912 | tf_op jit(solution)/shard_map/convert_element_type | solution.py:169
  273.2 10.8 %scatter_fusion.1 = f32[2,2,64,1024]{3,2,1,0:T(8,128)S(1)} fusion(f32[2,2,64,1024]{3,2,1,0:T(8,128)S(1)} %broadcast_in_dim.50, s32[16]{0:T(128)S(1)} %fusion.35, f32[16,2,64,1024]{3,2,1,0:T(8,128)} %bitcast_convert_fusion), kind=kCustom, calls=%fused_computation.4 | custom fusion | flops 2097152 | bytes 25165888 | tf_op jit(solution)/shard_map/scatter-add | solution.py:169
  285.0 11.9 %reduce_sum.62 = f32[2,128,1024]{2,1,0:T(8,128)S(1)} reduce(f32[32,2,128,1024]{3,2,1,0:T(8,128)} %all-gather.2.cloned.1.call-done, f32[]{:T(128)} %constant.77.clone.1), dimensions={0}, to_apply=%region_8.9 | reduce | flops 8126464 | bytes 34603012 | tf_op jit(solution)/shard_map/reduce_sum | solution.py:14
  (138 shorter events, 36.0 us)
Async XLA Ops:
  7.2 277.8 %all-gather.2.cloned.1.call-start = ((), (), s32[]{:S(2)}) async-start(), calls=%async_computation.3 | async-start | bytes 34603008 | tf_op jit(solution)/shard_map/all_gather | solution.py:13
  9.9 121.7 %copy-start.2 = (bf16[2,64,16,64]{3,2,1,0:T(8,128)(2,1)}, bf16[2,64,16,64]{3,2,1,0:T(8,128)(2,1)S(1)}, u32[]{:S(2)}) copy-start(bf16[2,64,16,64]{3,2,1,0:T(8,128)(2,1)S(1)} %reshape.258) | copy-start | bytes 786436
  9.9 2.7 copy-start.22
  10.8 2.0 copy-start.23
  15.5 1.4 copy-start.24
  15.6 1.6 copy-start.25
  15.6 8.4 %copy-start.20 = (bf16[1,128,1024]{2,1,0:T(8,128)(2,1)S(1)}, bf16[1,128,1024]{2,1,0:T(8,128)(2,1)}, u32[]{:S(2)}) copy-start(bf16[1,128,1024]{2,1,0:T(8,128)(2,1)} %param.15) | copy-start | bytes 786436
  15.6 8.4 %copy-start.21 = (bf16[1,128,1024]{2,1,0:T(8,128)(2,1)S(1)}, bf16[1,128,1024]{2,1,0:T(8,128)(2,1)}, u32[]{:S(2)}) copy-start(bf16[1,128,1024]{2,1,0:T(8,128)(2,1)} %param.16) | copy-start | bytes 786436
  18.8 9.8 %all-to-all-start = ((s32[8,1,2]{2,1,0:T(1,128)}), s32[8,1,2]{2,1,0:T(1,128)S(1)}, u32[]{:S(2)}, u32[]{:S(2)}) async-start(s32[8,1,2]{2,1,0:T(1,128)} %bitcast.12), calls=%async_computation | async-start | bytes 8192 | tf_op jit(solution)/shard_map/all_to_all | solution.py:139
  31.6 104.4 %all-to-all-start.1 = ((bf16[8,2,2,64,1024]{4,3,2,1,0:T(8,128)(2,1)}), bf16[8,2,2,64,1024]{4,3,2,1,0:T(8,128)(2,1)}, u32[]{:S(2)}, u32[]{:S(2)}) async-start(bf16[8,2,2,64,1024]{4,3,2,1,0:T(8,128)(2,1)} %bitcast.107), calls=%async_computation.1 | async-start | bytes 8388608 | tf_op jit(solution)/shard_map/all_to_all | solution.py:142
  36.2 81.0 %collective-permute-start = (bf16[2,64,1024]{2,1,0:T(8,128)(2,1)S(1)}, bf16[2,64,1024]{2,1,0:T(8,128)(2,1)}, u32[]{:S(2)}, u32[]{:S(2)}) collective-permute-start(bf16[2,64,1024]{2,1,0:T(8,128)(2,1)S(1)} %get-tuple-element.62), channel_id=1, source_target_pairs={{0,1},{1,2},{2,3},{3,4},{4,5},{5,6},{6,7},{7,0},{8,9},{9,10},{10,1... | collective-permute-start | bytes 786440 | tf_op jit(solution)/shard_map/ppermute | solution.py:23
  36.7 80.6 %collective-permute-start.1 = (bf16[2,64,1024]{2,1,0:T(8,128)(2,1)S(1)}, bf16[2,64,1024]{2,1,0:T(8,128)(2,1)}, u32[]{:S(2)}, u32[]{:S(2)}) collective-permute-start(bf16[2,64,1024]{2,1,0:T(8,128)(2,1)S(1)} %get-tuple-element.63), channel_id=1, source_target_pairs={{1,0},{2,1},{3,2},{4,3},{5,4},{6,5},{7,6},{0,7},{9,8},{10,9},{11,1... | collective-permute-start | bytes 786440 | tf_op jit(solution)/shard_map/ppermute | solution.py:26
  131.2 1.4 copy-start.9
  131.6 1.6 copy-start
  152.7 1.0 copy-start.19
  153.3 1.8 copy-start.4
  154.1 1.0 copy-start.18
  155.6 1.2 copy-start.8
  156.7 1.2 copy-start.6
  165.7 2.2 copy-start.17
  175.5 4.8 %copy-start.11 = (f32[2,192,16,64]{1,3,2,0:T(8,128)S(1)}, f32[2,192,16,64]{1,3,2,0:T(8,128)}, u32[]{:S(2)}) copy-start(f32[2,192,16,64]{1,3,2,0:T(8,128)} %multiply_bitcast_fusion) | copy-start | bytes 4718596
  175.5 90.4 %all-to-all-start.2 = ((bf16[8,2,2,64,1024]{4,3,2,1,0:T(8,128)(2,1)}), bf16[8,2,2,64,1024]{4,3,2,1,0:T(8,128)(2,1)}, u32[]{:S(2)}, u32[]{:S(2)}) async-start(bf16[8,2,2,64,1024]{4,3,2,1,0:T(8,128)(2,1)} %bitcast.106), calls=%async_computation.2 | async-start | bytes 8388608 | tf_op jit(solution)/shard_map/all_to_all | solution.py:158
  183.2 2.9 copy-start.1
  183.2 2.9 copy-start.3
  190.0 2.1 copy-start.16
  192.3 3.0 copy-start.10
  192.3 3.0 copy-start.13
  192.4 69.5 %collective-permute-start.2 = (f32[2,64,1024]{2,1,0:T(8,128)S(1)}, f32[2,64,1024]{2,1,0:T(8,128)S(1)}, u32[]{:S(2)}, u32[]{:S(2)}) collective-permute-start(f32[2,64,1024]{2,1,0:T(8,128)S(1)} %get-tuple-element.47), channel_id=1, source_target_pairs={{0,1},{1,2},{2,3},{3,4},{4,5},{5,6},{6,7},{7,0},{8,9},{9,10},{10,1... | collective-permute-start | bytes 1572872 | tf_op jit(solution)/shard_map/ppermute | solution.py:23
  193.0 69.0 %collective-permute-start.3 = (f32[2,64,1024]{2,1,0:T(8,128)S(1)}, f32[2,64,1024]{2,1,0:T(8,128)S(1)}, u32[]{:S(2)}, u32[]{:S(2)}) collective-permute-start(f32[2,64,1024]{2,1,0:T(8,128)S(1)} %get-tuple-element.46), channel_id=1, source_target_pairs={{1,0},{2,1},{3,2},{4,3},{5,4},{6,5},{7,6},{0,7},{9,8},{10,9},{11,1... | collective-permute-start | bytes 1572872 | tf_op jit(solution)/shard_map/ppermute | solution.py:26
  195.7 66.5 %copy-start.5 = (bf16[6,1,64,16,64]{4,3,2,1,0:T(8,128)(2,1)S(1)}, bf16[6,1,64,16,64]{4,3,2,1,0:T(8,128)(2,1)}, u32[]{:S(2)}) copy-start(bf16[6,1,64,16,64]{4,3,2,1,0:T(8,128)(2,1)} %copy-done.4) | copy-start | bytes 2359300
  195.7 66.5 %copy-start.7 = (bf16[6,16,64,64]{3,2,1,0:T(8,128)(2,1)S(1)}, bf16[6,16,64,64]{3,2,1,0:T(8,128)(2,1)}, u32[]{:S(2)}) copy-start(bf16[6,16,64,64]{3,2,1,0:T(8,128)(2,1)} %copy-done.6) | copy-start | bytes 2359300
  263.0 1.0 copy-start.15
  (2 other events, 1.8 us)
Sparse Core Ops, SparseCore 0:
  17.1 257.4 all-gather.1
